TPU v7x, 32 devices: a whole 2x2x4 slice. The times are simulated.
32 devices in a mesh: groups: 2 (over x), row: 4 (over y, core), col: 4 (over z).
Axes of the slice: x: 2, y: 2, z: 4, core: 2. Of those that a mesh axis runs over, the one named last changes fastest.
Arguments:
- observed: float32 [2048, 2048], P(('groups', 'row'), 'col'), parts along dimension 0, may hold values from -24 to 24
- estimate: float32 [2048, 2048], P(('groups', 'row'), 'col'), parts along dimension 0, may hold values from -6 to 6
- kernel: float32 [512, 256], P(('groups', 'row')), parts along dimension 0, may hold values from -6 to 6
Outputs:
- refined: float32 [2048, 2048], P(('groups', 'row'), 'col'), parts along dimension 0
- new_kernel: float32 [512, 256], P(('groups', 'row')), parts along dimension 0
There are 2 independent parts, one for each index of `groups`. A program takes and returns all parts, laid end to end along the dimension named above; each array names one. Nothing has to cross between parts.
All inputs are finite; a program needn't handle non-finite values.
Results may differ from a plain program's by a relative error of at most 0.0001.
Values sent between devices are 32-bit elements; how exact they have to be, the bound alone decides.
A program may use at most 128 MiB of HBM per device.

v0:
```python
import math
import jax
import jax.numpy as jnp
from jax import lax
from jax.sharding import PartitionSpec as P

HIGHEST = lax.Precision.HIGHEST
EPSILON = 1e-06


def padded(block, sides, width):
    for axis, dim in sides:
        count = lax.axis_size(axis)
        forward = [(i, i + 1) for i in range(count - 1)]
        backward = [(target, source) for source, target in forward]
        low = lax.ppermute(
            lax.slice_in_dim(block, block.shape[dim] - width, None, axis=dim), axis, forward
        )
        high = lax.ppermute(lax.slice_in_dim(block, 0, width, axis=dim), axis, backward)
        block = jnp.concatenate([low, block, high], axis=dim)
    return block


def tables(places, length):
    freqs = jnp.arange(length, dtype=jnp.int32)
    phase = jnp.mod(places[:, None] * freqs[None, :], length).astype(jnp.float32) * (
        2.0 * math.pi / length
    )
    return (jnp.cos(phase), jnp.sin(phase))


def forward(field, row_tables, col_tables):
    rows_long = row_tables[0].shape[1]
    cols_long = col_tables[0].shape[1]
    across = jnp.dot(field, jnp.concatenate(col_tables, 1), precision=HIGHEST)
    stacked = lax.dot_general(
        jnp.concatenate(row_tables, 1), across, (((0,), (0,)), ((), ())), precision=HIGHEST
    )
    real_part = stacked[:rows_long, :cols_long] - stacked[rows_long:, cols_long:]
    imag_part = -(stacked[rows_long:, :cols_long] + stacked[:rows_long, cols_long:])
    return (real_part, imag_part)


def inverse(real_part, imag_part, row_tables, col_tables):
    rows_long, cols_long = real_part.shape
    out_rows = row_tables[0].shape[0]
    stacked = jnp.dot(
        jnp.concatenate(row_tables, 0),
        jnp.concatenate([real_part, imag_part], 1),
        precision=HIGHEST,
    )
    mixed_re = stacked[:out_rows, :cols_long] - stacked[out_rows:, cols_long:]
    mixed_im = stacked[out_rows:, :cols_long] + stacked[:out_rows, cols_long:]
    result = lax.dot_general(
        jnp.concatenate([mixed_re, mixed_im], 1),
        jnp.concatenate([col_tables[0], -col_tables[1]], 1),
        (((1,), (1,)), ((), ())),
        precision=HIGHEST,
    )
    return result / (rows_long * cols_long)


def collect(kernel):
    return lax.all_gather(kernel, "row", axis=0, tiled=True)


def per_device(observed, estimate, kernel):
    tile_rows, tile_cols = observed.shape
    owner_rows, kernel_side = kernel.shape
    margin = kernel_side // 2
    rows_long = tile_rows + kernel_side
    cols_long = tile_cols + kernel_side
    factor = 1.0 / kernel_side
    ext_rows = tables(jnp.arange(rows_long, dtype=jnp.int32), rows_long)
    ext_cols = tables(jnp.arange(cols_long, dtype=jnp.int32), cols_long)
    own_rows = tables(jnp.arange(tile_rows, dtype=jnp.int32) + margin, rows_long)
    own_cols = tables(jnp.arange(tile_cols, dtype=jnp.int32) + margin, cols_long)
    lag_rows = tables(jnp.arange(kernel_side, dtype=jnp.int32) - margin, rows_long)
    lag_cols = tables(jnp.arange(kernel_side, dtype=jnp.int32) - margin, cols_long)
    image = estimate
    owned = kernel
    full_kernel = collect(kernel)
    widened = padded(image, (("row", 0), ("col", 1)), margin)
    image_re, image_im = forward(widened, ext_rows, ext_cols)
    kernel_re, kernel_im = forward(full_kernel, lag_rows, lag_cols)
    predicted = (
        inverse(
            image_re * kernel_re - image_im * kernel_im,
            image_re * kernel_im + image_im * kernel_re,
            own_rows,
            own_cols,
        )
        * factor
    )
    residual = predicted - observed
    local_squares = jnp.sum(residual * residual)
    loss = 0.5 * lax.psum(local_squares, ("row", "col"))
    wide_residual = padded(residual, (("row", 0), ("col", 1)), margin)
    resid_re, resid_im = forward(wide_residual, ext_rows, ext_cols)
    image_grad = (
        inverse(
            resid_re * kernel_re + resid_im * kernel_im,
            resid_im * kernel_re - resid_re * kernel_im,
            own_rows,
            own_cols,
        )
        * factor
    )
    tile_re, tile_im = forward(residual, own_rows, own_cols)
    kernel_grad = (
        inverse(
            tile_re * image_re + tile_im * image_im,
            tile_im * image_re - tile_re * image_im,
            lag_rows,
            lag_cols,
        )
        * factor
    )
    grad_squares = jnp.sum(image_grad * image_grad)
    image_norm = lax.psum(grad_squares, ("row", "col"))
    owner_grad = lax.psum_scatter(kernel_grad, "row", scatter_dimension=0, tiled=True)
    owner_grad = lax.psum(owner_grad, "col")
    kernel_norm = lax.psum(jnp.sum(owner_grad * owner_grad), "row")
    owned = owned - 0.25 * loss / (kernel_norm + EPSILON) * owner_grad
    image = image - loss / (image_norm + EPSILON) * image_grad
    return (image, owned)


def solution(mesh):
    placed = (P(("groups", "row"), "col"), P(("groups", "row"), "col"), P(("groups", "row"), None))
    return jax.shard_map(
        per_device,
        mesh=mesh,
        in_specs=placed,
        out_specs=(P(("groups", "row"), "col"), P(("groups", "row"), None)),
        check_vma=False,
    )
```

profile of v0, /device:TPU:0, one launch (start us, length us, event | category | flops | bytes accessed | tf_op | source)
XLA Modules:
  0.0 264.5 jit_solution(6838239969392656546)
XLA Ops:
  8.3 2.4 collective-permute-start
  12.0 4.3 %fusion.109 = (f32[256,768]{1,0:T(8,128)}, f32[256,768]{1,0:T(8,128)S(1)}, f32[256,768]{1,0:T(8,128)S(1)}) fusion(s32[256]{0:T(256)S(1)} %iota_add_fusion.1), kind=kLoop, calls=%fused_computation.148 | loop fusion | flops 1966080 | bytes 2360320 | tf_op jit(solution)/shard_map/neg | solution.py:56
  16.2 2.1 fusion.111
  18.4 9.1 %all_gather.3 = f32[256,256]{1,0:T(8,128)S(1)} all-gather(f32[64,256]{1,0:T(8,128)S(1)} %copy-done.28), channel_id=1, replica_groups=mesh['groups'=2,'row'=4,'col'=4] {'row'}, dimensions={0}, use_global_device_ids=true | all-gather | bytes 327680 | tf_op jit(solution)/shard_map/all_gather | solution.py:64
  27.5 8.3 %fusion.58 = (f32[512,768]{1,0:T(8,128)}, f32[512,768]{1,0:T(8,128)}, f32[512,768]{1,0:T(8,128)S(1)}) fusion(s32[512]{0:T(512)S(1)} %iota_add_fusion), kind=kLoop, calls=%fused_computation.80 | loop fusion | flops 3932160 | bytes 4720640 | tf_op jit(solution)/shard_map/sin | solution.py:29
  35.9 2.7 %fusion.27 = f32[1536,256]{1,0:T(8,128)S(1)} fusion(f32[256,256]{1,0:T(8,128)S(1)} %all_gather.3, f32[256,768]{1,0:T(8,128)S(1)} %get-tuple-element.32, f32[256,768]{1,0:T(8,128)S(1)} %get-tuple-element.31), kind=kOutput, calls=%fused_computation.36 | convolution fusion | flops 1208352768 | bytes 3407872 | tf_op jit(solution)/shard_map/dot_general | solution.py:35
  38.6 11.0 %fusion.64 = f32[1024,1536]{1,0:T(8,128)S(1)} fusion(f32[1536,256]{1,0:T(8,128)S(1)} %fusion.27, f32[256,512]{1,0:T(8,128)S(1)} %get-tuple-element.36, f32[256,512]{1,0:T(8,128)S(1)} %get-tuple-element.35), kind=kOutput, calls=%fused_computation.93 | convolution fusion | flops 4832100352 | bytes 8912896 | tf_op jit(solution)/shard_map/dot_general | solution.py:36
  49.6 9.5 %fusion.22 = (f32[768,768]{1,0:T(8,128)S(1)}, f32[768,768]{1,0:T(8,128)S(1)}) fusion(), kind=kLoop, calls=%fused_computation.28 | loop fusion | flops 5308416 | bytes 4718592 | tf_op jit(solution)/shard_map/sin | solution.py:29
  59.1 4.5 %fusion.103 = (f32[512,512]{1,0:T(8,128)S(1)}, f32[512,512]{1,0:T(8,128)S(1)}) fusion(), kind=kLoop, calls=%fused_computation.142 | loop fusion | flops 3670016 | bytes 2097152 | tf_op jit(solution)/shard_map/sin | solution.py:29
  63.8 3.5 %collective-permute-start.2 = (f32[512,128]{1,0:T(8,128)S(1)}, f32[512,128]{1,0:T(8,128)S(1)}, u32[]{:S(2)}, u32[]{:S(2)}) collective-permute-start(f32[512,128]{1,0:T(8,128)S(1)} %get-tuple-element.21), channel_id=1, source_target_pairs={{0,1},{1,2},{2,3},{4,5},{5,6},{6,7},{8,9},{9,10},{10,11},{12,13},{... | collective-permute-start | bytes 786440 | tf_op jit(solution)/shard_map/ppermute | solution.py:16
  68.6 3.2 %fusion.113 = (f32[256,512]{1,0:T(8,128)}, f32[256,512]{1,0:T(8,128)}) fusion(s32[256]{0:T(256)S(1)} %iota_add_fusion.2), kind=kLoop, calls=%fused_computation.155 | loop fusion | flops 1835008 | bytes 1049600 | tf_op jit(solution)/shard_map/cos | solution.py:29
  73.3 4.1 %collective-permute-done.3 = f32[512,128]{1,0:T(8,128)S(1)} collective-permute-done((f32[512,128]{1,0:T(8,128)S(1)}, f32[512,128]{1,0:T(8,128)S(1)}, u32[]{:S(2)}, u32[]{:S(2)}) %collective-permute-start.3) | collective-permute-done | bytes 262176 | tf_op jit(solution)/shard_map/ppermute | solution.py:19
  77.5 7.7 %fusion.1 = f32[512,1536]{1,0:T(8,128)S(1)} fusion(f32[768,768]{1,0:T(8,128)S(1)} %get-tuple-element.41, f32[768,768]{1,0:T(8,128)S(1)} %get-tuple-element.42, f32[512,128]{1,0:T(8,128)S(1)} %collective-permute-done.3, f32[512,512]{1,0:T(8,128)S(1)} %constant_dynamic-update-slice_fusion, f32[512,128]{1,0:T(8,128)S(1)} %collective-permute-done.2), kind=kOutput, calls=%fused_computation.2 | convolution fusion | flops 7249723392 | bytes 9437184 | tf_op jit(solution)/shard_map/dot_general | solution.py:35
  85.2 11.2 %fusion.26 = f32[1024,1536]{1,0:T(8,128)S(1)} fusion(f32[512,1536]{1,0:T(8,128)S(1)} %fusion.1, f32[512,512]{1,0:T(8,128)S(1)} %get-tuple-element.43, f32[512,512]{1,0:T(8,128)S(1)} %get-tuple-element.44), kind=kOutput, calls=%fused_computation.35 | convolution fusion | flops 9664200704 | bytes 11534336 | tf_op jit(solution)/shard_map/dot_general | solution.py:36
  96.4 3.1 %multiply_subtract_fusion.2 = (f32[512,768]{1,0:T(8,128)}, f32[512,768]{1,0:T(8,128)}, f32[512,768]{1,0:T(8,128)}, f32[512,768]{1,0:T(8,128)S(1)}, f32[512,768]{1,0:T(8,128)}) fusion(f32[1024,1536]{1,0:T(8,128)S(1)} %fusion.26, f32[1024,1536]{1,0:T(8,128)S(1)} %fusion.64), kind=kLoop, calls=%fused_computation.83 | loop fusion | flops 2752512 | bytes 20447232 | tf_op jit(solution)/shard_map/sub | solution.py:88
  99.5 2.9 %multiply_add_fusion.2 = f32[512,768]{1,0:T(8,128)S(1)} fusion(f32[512,768]{1,0:T(8,128)} %get-tuple-element.8, f32[512,768]{1,0:T(8,128)} %get-tuple-element.6, f32[512,768]{1,0:T(8,128)} %get-tuple-element.5, f32[512,768]{1,0:T(8,128)S(1)} %get-tuple-element.7), kind=kLoop, calls=%fused_computation.82 | loop fusion | flops 1966080 | bytes 7864320 | tf_op jit(solution)/shard_map/add | solution.py:89
  102.7 5.4 %fusion.3 = f32[512,1536]{1,0:T(8,128)S(1)} fusion(f32[512,768]{1,0:T(8,128)S(1)} %multiply_add_fusion.2, f32[512,768]{1,0:T(8,128)S(1)} %copy-done.16, f32[256,512]{1,0:T(8,128)S(1)} %copy-done.11, f32[256,512]{1,0:T(8,128)S(1)} %copy-done.9), kind=kOutput, calls=%fused_computation.7 | convolution fusion | flops 4832886784 | bytes 7340032 | tf_op jit(solution)/shard_map/dot_general | solution.py:47
  109.6 3.7 %multiply_reduce_fusion.1 = (f32[]{:T(128)}, f32[256,512]{1,0:T(8,128)S(1)}) fusion(f32[256,512]{1,0:T(8,128)S(1)} %copy-done.27, f32[512,768]{1,0:T(8,128)S(1)} %get-tuple-element.29, f32[512,768]{1,0:T(8,128)S(1)} %copy-done.3, f32[256,768]{1,0:T(8,128)S(1)} %get-tuple-element.18, f32[256,768]{1,0:T(8,128)S(1)} %get-tuple-element.17), kind=kOutput, calls=%fused_computation.139 | convolution fusion | flops 2417623040 | bytes 5767172 | tf_op jit(solution)/shard_map/dot_general | solution.py:54
  113.4 2.8 %fusion.2 = f32[256,1536]{1,0:T(8,128)S(1)} fusion(f32[256,512]{1,0:T(8,128)S(1)} %get-tuple-element.38, f32[512,768]{1,0:T(8,128)S(1)} %get-tuple-element.29, f32[512,768]{1,0:T(8,128)S(1)} %copy-done.17), kind=kOutput, calls=%fused_computation.6 | convolution fusion | flops 2416705536 | bytes 5242880 | tf_op jit(solution)/shard_map/dot_general | solution.py:35
  116.2 5.6 %fusion.71 = f32[1024,1536]{1,0:T(8,128)S(1)} fusion(f32[256,1536]{1,0:T(8,128)S(1)} %fusion.2, f32[256,512]{1,0:T(8,128)S(1)} %copy-done.11, f32[256,512]{1,0:T(8,128)S(1)} %copy-done.9), kind=kOutput, calls=%fused_computation.100 | convolution fusion | flops 4832100352 | bytes 8912896 | tf_op jit(solution)/shard_map/dot_general | solution.py:36
  123.1 1.8 collective-permute-start.5
  125.6 5.4 %fusion.12 = f32[512,1536]{1,0:T(8,128)S(1)} fusion(f32[512,768]{1,0:T(8,128)S(1)} %get-tuple-element.10, f32[512,768]{1,0:T(8,128)S(1)} %get-tuple-element.9, f32[256,512]{1,0:T(8,128)S(1)} %copy-done.23, f32[256,512]{1,0:T(8,128)S(1)} %copy-done.21), kind=kOutput, calls=%fused_computation.16 | convolution fusion | flops 4832886784 | bytes 7340032 | tf_op jit(solution)/shard_map/dot_general | solution.py:47
  132.0 4.2 %collective-permute-start.6 = (f32[512,128]{1,0:T(8,128)}, f32[512,128]{1,0:T(8,128)}, u32[]{:S(2)}, u32[]{:S(2)}) collective-permute-start(f32[512,128]{1,0:T(8,128)} %get-tuple-element.19), channel_id=1, source_target_pairs={{0,1},{1,2},{2,3},{4,5},{5,6},{6,7},{8,9},{9,10},{10,11},{12,13},{... | collective-permute-start | bytes 786440 | tf_op jit(solution)/shard_map/ppermute | solution.py:16
  137.8 2.2 fusion.91
  140.4 5.5 %collective-permute-done.7 = f32[512,128]{1,0:T(8,128)} collective-permute-done((f32[512,128]{1,0:T(8,128)}, f32[512,128]{1,0:T(8,128)}, u32[]{:S(2)}, u32[]{:S(2)}) %collective-permute-start.7) | collective-permute-done | bytes 262176 | tf_op jit(solution)/shard_map/ppermute | solution.py:19
  145.9 10.4 %fusion = f32[512,1536]{1,0:T(8,128)S(1)} fusion(f32[768,768]{1,0:T(8,128)} %copy-done.25, f32[768,768]{1,0:T(8,128)} %copy-done.26, f32[512,128]{1,0:T(8,128)} %collective-permute-done.7, f32[128,512]{1,0:T(8,128)} %copy-done.29, f32[256,512]{1,0:T(8,128)} %copy-done.13, f32[128,512]{1,0:T(8,128)S(1)} %collective-permute-done.4, ...), kind=kOutput, calls=%fused_computation.1 | convolution fusion | flops 7250509824 | bytes 9437184 | tf_op jit(solution)/shard_map/dot_general | solution.py:35
  156.4 10.9 %fusion.25 = f32[1024,1536]{1,0:T(8,128)S(1)} fusion(f32[512,1536]{1,0:T(8,128)S(1)} %fusion, f32[512,512]{1,0:T(8,128)S(1)} %copy-done.6, f32[512,512]{1,0:T(8,128)S(1)} %copy-done.8), kind=kOutput, calls=%fused_computation.34 | convolution fusion | flops 9664200704 | bytes 11534336 | tf_op jit(solution)/shard_map/dot_general | solution.py:36
  168.5 5.6 %fusion.7 = f32[512,1536]{1,0:T(8,128)S(1)} fusion(f32[512,768]{1,0:T(8,128)S(1)} %get-tuple-element.12, f32[512,768]{1,0:T(8,128)S(1)} %get-tuple-element.11, f32[256,512]{1,0:T(8,128)S(1)} %copy-done.12, f32[256,512]{1,0:T(8,128)S(1)} %copy-done.10), kind=kOutput, calls=%fused_computation.11 | convolution fusion | flops 4832886784 | bytes 7340032 | tf_op jit(solution)/shard_map/dot_general | solution.py:47
  175.5 3.5 %multiply_reduce_fusion = (f32[]{:T(128)}, f32[256,512]{1,0:T(8,128)S(1)}) fusion(f32[512,768]{1,0:T(8,128)S(1)} %get-tuple-element.29, f32[512,768]{1,0:T(8,128)S(1)} %copy-done.4, f32[256,768]{1,0:T(8,128)S(1)} %get-tuple-element.16, f32[256,768]{1,0:T(8,128)S(1)} %get-tuple-element.15), kind=kOutput, calls=%fused_computation.138 | convolution fusion | flops 2417491968 | bytes 5242884 | tf_op jit(solution)/shard_map/dot_general | solution.py:54
  179.0 31.2 %all-reduce = (f32[]{:T(128)}, f32[]{:T(128)}) all-reduce(f32[]{:T(128)} %get-tuple-element.37, f32[]{:T(128)} %get-tuple-element.39), channel_id=1, replica_groups=mesh['groups'=2,'row'=4,'col'=4] {'row','col'}, use_global_device_ids=true, to_apply=%region_1.2 | all-reduce | flops 2 | bytes 16 | tf_op jit(solution)/shard_map/psum | solution.py:97
  212.5 34.5 %all-reduce.3.cloned.1.call-done = f32[64,256]{1,0:T(8,128)} async-done(((f32[64,256]{1,0:T(8,128)}), f32[64,256]{1,0:T(8,128)}) %all-reduce.3.cloned.1.call-update) | async-done | bytes 65552 | tf_op jit(solution)/shard_map/psum | solution.py:122
  249.1 6.2 %psum.31 = f32[]{:T(128)} all-reduce(f32[]{:T(128)} %multiply_reduce_fusion.2), channel_id=1, replica_groups=mesh['groups'=2,'row'=4,'col'=4] {'row'}, use_global_device_ids=true, to_apply=%region_7.8 | all-reduce | flops 1 | bytes 8 | tf_op jit(solution)/shard_map/psum | solution.py:123
  (93 shorter events, 18.5 us)
Async XLA Ops:
  7.2 204.4 %reduce-scatter.2.cloned.1.call-start = ((), (), s32[]{:S(2)}) async-start(), calls=%async_computation.1 | async-start | bytes 327680 | tf_op jit(solution)/shard_map/reduce_scatter | solution.py:121
  8.3 55.3 %collective-permute-start = (f32[128,512]{1,0:T(8,128)S(1)}, f32[128,512]{1,0:T(8,128)S(1)}, u32[]{:S(2)}, u32[]{:S(2)}) collective-permute-start(f32[128,512]{1,0:T(8,128)S(1)} %get-tuple-element.26), channel_id=1, source_target_pairs={{0,4},{4,8},{8,12},{1,5},{5,9},{9,13},{2,6},{6,10},{10,14},{3,7},{... | collective-permute-start | bytes 786440 | tf_op jit(solution)/shard_map/ppermute | solution.py:16
  10.7 53.0 %collective-permute-start.1 = (f32[128,512]{1,0:T(8,128)S(1)}, f32[128,512]{1,0:T(8,128)S(1)}, u32[]{:S(2)}, u32[]{:S(2)}) collective-permute-start(f32[128,512]{1,0:T(8,128)S(1)} %get-tuple-element.25), channel_id=1, source_target_pairs={{4,0},{8,4},{12,8},{5,1},{9,5},{13,9},{6,2},{10,6},{14,10},{7,3},{... | collective-permute-start | bytes 786440 | tf_op jit(solution)/shard_map/ppermute | solution.py:19
  12.0 6.4 %copy-start.28 = (f32[64,256]{1,0:T(8,128)S(1)}, f32[64,256]{1,0:T(8,128)}, u32[]{:S(2)}) copy-start(f32[64,256]{1,0:T(8,128)} %param.5) | copy-start | bytes 196612
  16.2 19.6 %copy-start.14 = (f32[256,768]{1,0:T(8,128)}, f32[256,768]{1,0:T(8,128)S(1)}, u32[]{:S(2)}) copy-start(f32[256,768]{1,0:T(8,128)S(1)} %get-tuple-element.32) | copy-start | bytes 2359300
  18.4 20.2 %copy-start.20 = (f32[256,512]{1,0:T(8,128)}, f32[256,512]{1,0:T(8,128)S(1)}, u32[]{:S(2)}) copy-start(f32[256,512]{1,0:T(8,128)S(1)} %get-tuple-element.35) | copy-start | bytes 1572868
  18.4 20.2 %copy-start.22 = (f32[256,512]{1,0:T(8,128)}, f32[256,512]{1,0:T(8,128)S(1)}, u32[]{:S(2)}) copy-start(f32[256,512]{1,0:T(8,128)S(1)} %get-tuple-element.36) | copy-start | bytes 1572868
  59.1 18.4 %copy-start.25 = (f32[768,768]{1,0:T(8,128)}, f32[768,768]{1,0:T(8,128)S(1)}, u32[]{:S(2)}) copy-start(f32[768,768]{1,0:T(8,128)S(1)} %get-tuple-element.41) | copy-start | bytes 7077892
  59.1 18.4 %copy-start.26 = (f32[768,768]{1,0:T(8,128)}, f32[768,768]{1,0:T(8,128)S(1)}, u32[]{:S(2)}) copy-start(f32[768,768]{1,0:T(8,128)S(1)} %get-tuple-element.42) | copy-start | bytes 7077892
  59.1 4.6 %copy-start.18 = (f32[256,512]{1,0:T(8,128)S(1)}, f32[256,512]{1,0:T(8,128)}, u32[]{:S(2)}) copy-start(f32[256,512]{1,0:T(8,128)} %param.4) | copy-start | bytes 1572868
  63.6 21.6 %copy-start.5 = (f32[512,512]{1,0:T(8,128)}, f32[512,512]{1,0:T(8,128)S(1)}, u32[]{:S(2)}) copy-start(f32[512,512]{1,0:T(8,128)S(1)} %get-tuple-element.43) | copy-start | bytes 3145732
  63.6 21.6 %copy-start.7 = (f32[512,512]{1,0:T(8,128)}, f32[512,512]{1,0:T(8,128)S(1)}, u32[]{:S(2)}) copy-start(f32[512,512]{1,0:T(8,128)S(1)} %get-tuple-element.44) | copy-start | bytes 3145732
  63.8 9.5 %collective-permute-start.2 = (f32[512,128]{1,0:T(8,128)S(1)}, f32[512,128]{1,0:T(8,128)S(1)}, u32[]{:S(2)}, u32[]{:S(2)}) collective-permute-start(f32[512,128]{1,0:T(8,128)S(1)} %get-tuple-element.21), channel_id=1, source_target_pairs={{0,1},{1,2},{2,3},{4,5},{5,6},{6,7},{8,9},{9,10},{10,11},{12,13},{... | collective-permute-start | bytes 786440 | tf_op jit(solution)/shard_map/ppermute | solution.py:16
  67.3 10.2 %collective-permute-start.3 = (f32[512,128]{1,0:T(8,128)S(1)}, f32[512,128]{1,0:T(8,128)S(1)}, u32[]{:S(2)}, u32[]{:S(2)}) collective-permute-start(f32[512,128]{1,0:T(8,128)S(1)} %get-tuple-element.22), channel_id=1, source_target_pairs={{1,0},{2,1},{3,2},{5,4},{6,5},{7,6},{9,8},{10,9},{11,10},{13,12},{... | collective-permute-start | bytes 786440 | tf_op jit(solution)/shard_map/ppermute | solution.py:19
  99.5 2.9 %copy-start.9 = (f32[256,512]{1,0:T(8,128)S(1)}, f32[256,512]{1,0:T(8,128)}, u32[]{:S(2)}) copy-start(f32[256,512]{1,0:T(8,128)} %get-tuple-element.33) | copy-start | bytes 1572868
  99.5 2.9 %copy-start.11 = (f32[256,512]{1,0:T(8,128)S(1)}, f32[256,512]{1,0:T(8,128)}, u32[]{:S(2)}) copy-start(f32[256,512]{1,0:T(8,128)} %get-tuple-element.34) | copy-start | bytes 1572868
  99.5 3.1 %copy-start.16 = (f32[512,768]{1,0:T(8,128)S(1)}, f32[512,768]{1,0:T(8,128)}, u32[]{:S(2)}) copy-start(f32[512,768]{1,0:T(8,128)} %get-tuple-element.4) | copy-start | bytes 4718596
  109.6 3.8 %copy-start.17 = (f32[512,768]{1,0:T(8,128)S(1)}, f32[512,768]{1,0:T(8,128)}, u32[]{:S(2)}) copy-start(f32[512,768]{1,0:T(8,128)} %get-tuple-element.27) | copy-start | bytes 4718596
  113.3 17.7 %copy-start.13 = (f32[256,512]{1,0:T(8,128)}, f32[256,512]{1,0:T(8,128)S(1)}, u32[]{:S(2)}) copy-start(f32[256,512]{1,0:T(8,128)S(1)} %get-tuple-element.38) | copy-start | bytes 1572868
  116.2 8.8 %copy-start.1 = (f32[512,768]{1,0:T(8,128)S(1)}, f32[512,768]{1,0:T(8,128)}, u32[]{:S(2)}) copy-start(f32[512,768]{1,0:T(8,128)} %get-tuple-element.5) | copy-start | bytes 4718596
  116.2 8.8 %copy-start.2 = (f32[512,768]{1,0:T(8,128)S(1)}, f32[512,768]{1,0:T(8,128)}, u32[]{:S(2)}) copy-start(f32[512,768]{1,0:T(8,128)} %get-tuple-element.6) | copy-start | bytes 4718596
  121.8 9.2 %collective-permute-start.4 = (f32[128,512]{1,0:T(8,128)S(1)}, f32[128,512]{1,0:T(8,128)S(1)}, u32[]{:S(2)}, u32[]{:S(2)}) collective-permute-start(f32[128,512]{1,0:T(8,128)S(1)} %get-tuple-element.23), channel_id=1, source_target_pairs={{0,4},{4,8},{8,12},{1,5},{5,9},{9,13},{2,6},{6,10},{10,14},{3,7},{... | collective-permute-start | bytes 786440 | tf_op jit(solution)/shard_map/ppermute | solution.py:16
  123.1 2.5 copy-start.21
  123.1 7.9 %collective-permute-start.5 = (f32[128,512]{1,0:T(8,128)S(1)}, f32[128,512]{1,0:T(8,128)S(1)}, u32[]{:S(2)}, u32[]{:S(2)}) collective-permute-start(f32[128,512]{1,0:T(8,128)S(1)} %get-tuple-element.24), channel_id=1, source_target_pairs={{4,0},{8,4},{12,8},{5,1},{9,5},{13,9},{6,2},{10,6},{14,10},{7,3},{... | collective-permute-start | bytes 786440 | tf_op jit(solution)/shard_map/ppermute | solution.py:19
  131.0 6.7 %copy-start.29 = (f32[128,512]{1,0:T(8,128)}, f32[128,512]{1,0:T(8,128)S(1)}, u32[]{:S(2)}) copy-start(f32[128,512]{1,0:T(8,128)S(1)} %collective-permute-done.5) | copy-start | bytes 786436
  132.0 8.5 %collective-permute-start.6 = (f32[512,128]{1,0:T(8,128)}, f32[512,128]{1,0:T(8,128)}, u32[]{:S(2)}, u32[]{:S(2)}) collective-permute-start(f32[512,128]{1,0:T(8,128)} %get-tuple-element.19), channel_id=1, source_target_pairs={{0,1},{1,2},{2,3},{4,5},{5,6},{6,7},{8,9},{9,10},{10,11},{12,13},{... | collective-permute-start | bytes 786440 | tf_op jit(solution)/shard_map/ppermute | solution.py:16
  136.1 9.8 %collective-permute-start.7 = (f32[512,128]{1,0:T(8,128)}, f32[512,128]{1,0:T(8,128)}, u32[]{:S(2)}, u32[]{:S(2)}) collective-permute-start(f32[512,128]{1,0:T(8,128)} %get-tuple-element.20), channel_id=1, source_target_pairs={{1,0},{2,1},{3,2},{5,4},{6,5},{7,6},{9,8},{10,9},{11,10},{13,12},{... | collective-permute-start | bytes 786440 | tf_op jit(solution)/shard_map/ppermute | solution.py:19
  140.0 107.1 %all-reduce.3.cloned.1.call-start = ((), (), s32[]{:S(2)}) async-start(), calls=%async_computation.2 | async-start | bytes 131072 | tf_op jit(solution)/shard_map/psum | solution.py:122
  140.0 16.3 %copy-start.6 = (f32[512,512]{1,0:T(8,128)S(1)}, f32[512,512]{1,0:T(8,128)}, u32[]{:S(2)}) copy-start(f32[512,512]{1,0:T(8,128)} %copy-done.5) | copy-start | bytes 3145732
  140.0 16.3 %copy-start.8 = (f32[512,512]{1,0:T(8,128)S(1)}, f32[512,512]{1,0:T(8,128)}, u32[]{:S(2)}) copy-start(f32[512,512]{1,0:T(8,128)} %copy-done.7) | copy-start | bytes 3145732
  156.4 10.9 %copy-start = (f32[512,768]{1,0:T(8,128)S(1)}, f32[512,768]{1,0:T(8,128)}, u32[]{:S(2)}) copy-start(f32[512,768]{1,0:T(8,128)} %get-tuple-element.8) | copy-start | bytes 4718596
  175.5 36.1 %copy-start.19 = (f32[256,512]{1,0:T(8,128)S(1)}, f32[256,512]{1,0:T(8,128)}, u32[]{:S(2)}) copy-start(f32[256,512]{1,0:T(8,128)} %param.4) | copy-start | bytes 1572868
  (8 other events, 12.3 us)
Sparse Core Ops, SparseCore 0:
  140.1 23.7 reduce-scatter.1
  211.7 35.2 all-reduce.2
where the time goes:
time: 269 us; the launch traced here: 265 us
  matrix products  88.1 us (33%)
  blocking collectives  46.5 us (17%)
  waiting for transfers between devices  46.1 us (17%)
  other arithmetic  44.6 us (17%)
  between operations  17.6 us (7%)
  starting transfers between devices  17.2 us (6%)
  local copies, waits for them, and re-layouts  4.45 us (2%)
    dot_general x4, matrix products, forward(): lax.dot_general(jnp.concatenate(row_tables, 1), across, (((0,), (0,)), ((...  38.7 us
    psum x1, waiting for transfers between devices, per_device(): owner_grad = lax.psum(owner_grad, 'col')  34.5 us
    psum x1, blocking collectives, per_device(): loss = 0.5 * lax.psum(local_squares, ('row', 'col'))  31.2 us
    dot_general x4, matrix products, forward(): across = jnp.dot(field, jnp.concatenate(col_tables, 1), precision=HIGHEST)  23.6 us
    sin x3, other arithmetic, tables(): return (jnp.cos(phase), jnp.sin(phase))  22.3 us
    dot_general x3, matrix products, inverse(): jnp.dot(jnp.concatenate(row_tables, 0), jnp.concatenate([real_part, imag_...  16.4 us
    ppermute x4, starting transfers between devices, padded(): lax.ppermute(lax.slice_in_dim(block, block.shape[dim] - width, None, axis...  11.3 us
    ppermute x4, waiting for transfers between devices, padded(): lax.ppermute(lax.slice_in_dim(block, 0, width, axis=dim), axis, backward)  9.63 us
  transfers between devices with their start and end apart: 10, of which 5 were waited for; matrix products, arithmetic and copies ran while one was open for 33% of the time, Pallas kernels for 0%

commit v1 on v0

--- a/solution.py
+++ b/solution.py
@@ -119,7 +119,7 @@
     grad_squares = jnp.sum(image_grad * image_grad)
     image_norm = lax.psum(grad_squares, ("row", "col"))
     owner_grad = lax.psum_scatter(kernel_grad, "row", scatter_dimension=0, tiled=True)
-    owner_grad = lax.psum(owner_grad, "col")
+    owner_grad = jnp.sum(lax.all_gather(owner_grad, "col"), axis=0)
     kernel_norm = lax.psum(jnp.sum(owner_grad * owner_grad), "row")
     owned = owned - 0.25 * loss / (kernel_norm + EPSILON) * owner_grad
     image = image - loss / (image_norm + EPSILON) * image_grad

time: 269 us -> 260 us (0.967)
  waiting for transfers between devices: 46.1 us -> 14.4 us
  blocking collectives: 46.5 us -> 63.2 us
  matrix products: 88.1 us -> 90.9 us
    psum x1 -> x0, waiting for transfers between devices: 34.5 us -> none  [per_device(): owner_grad = lax.psum(owner_grad, 'col')]
    all_gather x0 -> x1, blocking collectives: none -> 14.5 us  [per_device(): owner_grad = jnp.sum(lax.all_gather(owner_grad, 'col'), axis=0)]
    reduce_scatter x1, waiting for transfers between devices: 0.02 us -> 4.9 us  [per_device(): lax.psum_scatter(kernel_grad, 'row', scatter_dimension=0, tiled=True)]
  transfers between devices with their start and end apart: 10 -> 9, of which waited for: 5 -> 4; matrix products, arithmetic and copies ran while one was open for 33% -> 19% of each run, Pallas kernels for 0% -> 0%
where the time goes in v1:
time: 260 us; the launch traced here: 255 us
  matrix products  90.9 us (35%)
  blocking collectives  63.2 us (24%)
  other arithmetic  46.2 us (18%)
  between operations  17.4 us (7%)
  starting transfers between devices  16.5 us (6%)
  waiting for transfers between devices  14.4 us (6%)
  local copies, waits for them, and re-layouts  6.69 us (3%)
    dot_general x4, matrix products, forward(): lax.dot_general(jnp.concatenate(row_tables, 1), across, (((0,), (0,)), ((...  38.7 us
    psum x1, blocking collectives, per_device(): loss = 0.5 * lax.psum(local_squares, ('row', 'col'))  33.3 us
    dot_general x4, matrix products, forward(): across = jnp.dot(field, jnp.concatenate(col_tables, 1), precision=HIGHEST)  23.9 us
    sin x3, other arithmetic, tables(): return (jnp.cos(phase), jnp.sin(phase))  22.3 us
    dot_general x3, matrix products, inverse(): jnp.dot(jnp.concatenate(row_tables, 0), jnp.concatenate([real_part, imag_...  16.8 us
    all_gather x1, blocking collectives, per_device(): owner_grad = jnp.sum(lax.all_gather(owner_grad, 'col'), axis=0)  14.5 us
    dot_general x3, matrix products, inverse(): lax.dot_general(jnp.concatenate([mixed_re, mixed_im], 1), jnp.concatenate...  11.5 us
    ppermute x4, starting transfers between devices, padded(): lax.ppermute(lax.slice_in_dim(block, block.shape[dim] - width, None, axis...  11.3 us
  transfers between devices with their start and end apart: 9, of which 4 were waited for; matrix products, arithmetic and copies ran while one was open for 19% of the time, Pallas kernels for 0%

profile of v1, /device:TPU:0, one launch (start us, length us, event | category | flops | bytes accessed | tf_op | source)
XLA Modules:
  0.0 255.4 jit_solution(3134599679292049373)
XLA Ops:
  8.3 2.4 collective-permute-start
  12.0 4.2 %fusion.109 = (f32[256,768]{1,0:T(8,128)}, f32[256,768]{1,0:T(8,128)S(1)}, f32[256,768]{1,0:T(8,128)S(1)}) fusion(s32[256]{0:T(256)S(1)} %iota_add_fusion.1), kind=kLoop, calls=%fused_computation.148 | loop fusion | flops 1966080 | bytes 2360320 | tf_op jit(solution)/shard_map/neg | solution.py:56
  16.2 2.1 fusion.111
  18.4 9.1 %all_gather.9 = f32[256,256]{1,0:T(8,128)S(1)} all-gather(f32[64,256]{1,0:T(8,128)S(1)} %copy-done.27), channel_id=1, replica_groups=mesh['groups'=2,'row'=4,'col'=4] {'row'}, dimensions={0}, use_global_device_ids=true | all-gather | bytes 327680 | tf_op jit(solution)/shard_map/all_gather | solution.py:64
  27.5 8.3 %fusion.58 = (f32[512,768]{1,0:T(8,128)}, f32[512,768]{1,0:T(8,128)}, f32[512,768]{1,0:T(8,128)S(1)}) fusion(s32[512]{0:T(512)S(1)} %iota_add_fusion), kind=kLoop, calls=%fused_computation.80 | loop fusion | flops 3932160 | bytes 4720640 | tf_op jit(solution)/shard_map/sin | solution.py:29
  35.8 2.7 %fusion.27 = f32[1536,256]{1,0:T(8,128)S(1)} fusion(f32[256,256]{1,0:T(8,128)S(1)} %all_gather.9, f32[256,768]{1,0:T(8,128)S(1)} %get-tuple-element.32, f32[256,768]{1,0:T(8,128)S(1)} %get-tuple-element.31), kind=kOutput, calls=%fused_computation.36 | convolution fusion | flops 1208352768 | bytes 3407872 | tf_op jit(solution)/shard_map/dot_general | solution.py:35
  38.6 11.0 %fusion.64 = f32[1024,1536]{1,0:T(8,128)S(1)} fusion(f32[1536,256]{1,0:T(8,128)S(1)} %fusion.27, f32[256,512]{1,0:T(8,128)S(1)} %get-tuple-element.36, f32[256,512]{1,0:T(8,128)S(1)} %get-tuple-element.35), kind=kOutput, calls=%fused_computation.93 | convolution fusion | flops 4832100352 | bytes 8912896 | tf_op jit(solution)/shard_map/dot_general | solution.py:36
  49.6 9.5 %fusion.22 = (f32[768,768]{1,0:T(8,128)S(1)}, f32[768,768]{1,0:T(8,128)S(1)}) fusion(), kind=kLoop, calls=%fused_computation.28 | loop fusion | flops 5308416 | bytes 4718592 | tf_op jit(solution)/shard_map/sin | solution.py:29
  59.1 4.5 %fusion.103 = (f32[512,512]{1,0:T(8,128)S(1)}, f32[512,512]{1,0:T(8,128)S(1)}) fusion(), kind=kLoop, calls=%fused_computation.142 | loop fusion | flops 3670016 | bytes 2097152 | tf_op jit(solution)/shard_map/sin | solution.py:29
  63.8 3.5 %collective-permute-start.2 = (f32[512,128]{1,0:T(8,128)S(1)}, f32[512,128]{1,0:T(8,128)S(1)}, u32[]{:S(2)}, u32[]{:S(2)}) collective-permute-start(f32[512,128]{1,0:T(8,128)S(1)} %get-tuple-element.21), channel_id=1, source_target_pairs={{0,1},{1,2},{2,3},{4,5},{5,6},{6,7},{8,9},{9,10},{10,11},{12,13},{... | collective-permute-start | bytes 786440 | tf_op jit(solution)/shard_map/ppermute | solution.py:16
  68.6 3.2 %fusion.113 = (f32[256,512]{1,0:T(8,128)}, f32[256,512]{1,0:T(8,128)}) fusion(s32[256]{0:T(256)S(1)} %iota_add_fusion.2), kind=kLoop, calls=%fused_computation.155 | loop fusion | flops 1835008 | bytes 1049600 | tf_op jit(solution)/shard_map/cos | solution.py:29
  73.3 4.1 %collective-permute-done.3 = f32[512,128]{1,0:T(8,128)S(1)} collective-permute-done((f32[512,128]{1,0:T(8,128)S(1)}, f32[512,128]{1,0:T(8,128)S(1)}, u32[]{:S(2)}, u32[]{:S(2)}) %collective-permute-start.3) | collective-permute-done | bytes 262176 | tf_op jit(solution)/shard_map/ppermute | solution.py:19
  77.5 7.7 %fusion.1 = f32[512,1536]{1,0:T(8,128)S(1)} fusion(f32[768,768]{1,0:T(8,128)S(1)} %get-tuple-element.41, f32[768,768]{1,0:T(8,128)S(1)} %get-tuple-element.42, f32[512,128]{1,0:T(8,128)S(1)} %collective-permute-done.3, f32[512,512]{1,0:T(8,128)S(1)} %constant_dynamic-update-slice_fusion, f32[512,128]{1,0:T(8,128)S(1)} %collective-permute-done.2), kind=kOutput, calls=%fused_computation.2 | convolution fusion | flops 7249723392 | bytes 9437184 | tf_op jit(solution)/shard_map/dot_general | solution.py:35
  85.2 11.2 %fusion.26 = f32[1024,1536]{1,0:T(8,128)S(1)} fusion(f32[512,1536]{1,0:T(8,128)S(1)} %fusion.1, f32[512,512]{1,0:T(8,128)S(1)} %get-tuple-element.43, f32[512,512]{1,0:T(8,128)S(1)} %get-tuple-element.44), kind=kOutput, calls=%fused_computation.35 | convolution fusion | flops 9664200704 | bytes 11534336 | tf_op jit(solution)/shard_map/dot_general | solution.py:36
  96.4 3.1 %multiply_subtract_fusion.2 = (f32[512,768]{1,0:T(8,128)}, f32[512,768]{1,0:T(8,128)}, f32[512,768]{1,0:T(8,128)}, f32[512,768]{1,0:T(8,128)S(1)}, f32[512,768]{1,0:T(8,128)}) fusion(f32[1024,1536]{1,0:T(8,128)S(1)} %fusion.26, f32[1024,1536]{1,0:T(8,128)S(1)} %fusion.64), kind=kLoop, calls=%fused_computation.83 | loop fusion | flops 2752512 | bytes 20447232 | tf_op jit(solution)/shard_map/sub | solution.py:88
  99.5 2.9 %multiply_add_fusion.2 = f32[512,768]{1,0:T(8,128)S(1)} fusion(f32[512,768]{1,0:T(8,128)} %get-tuple-element.8, f32[512,768]{1,0:T(8,128)} %get-tuple-element.6, f32[512,768]{1,0:T(8,128)} %get-tuple-element.5, f32[512,768]{1,0:T(8,128)S(1)} %get-tuple-element.7), kind=kLoop, calls=%fused_computation.82 | loop fusion | flops 1966080 | bytes 7864320 | tf_op jit(solution)/shard_map/add | solution.py:89
  102.7 5.4 %fusion.3 = f32[512,1536]{1,0:T(8,128)S(1)} fusion(f32[512,768]{1,0:T(8,128)S(1)} %multiply_add_fusion.2, f32[512,768]{1,0:T(8,128)S(1)} %copy-done.16, f32[256,512]{1,0:T(8,128)S(1)} %copy-done.11, f32[256,512]{1,0:T(8,128)S(1)} %copy-done.9), kind=kOutput, calls=%fused_computation.7 | convolution fusion | flops 4832886784 | bytes 7340032 | tf_op jit(solution)/shard_map/dot_general | solution.py:47
  109.5 3.7 %multiply_reduce_fusion.1 = (f32[]{:T(128)}, f32[256,512]{1,0:T(8,128)S(1)}) fusion(f32[256,512]{1,0:T(8,128)S(1)} %copy-done.26, f32[512,768]{1,0:T(8,128)S(1)} %get-tuple-element.29, f32[512,768]{1,0:T(8,128)S(1)} %copy-done.3, f32[256,768]{1,0:T(8,128)S(1)} %get-tuple-element.18, f32[256,768]{1,0:T(8,128)S(1)} %get-tuple-element.17), kind=kOutput, calls=%fused_computation.139 | convolution fusion | flops 2417623040 | bytes 5767172 | tf_op jit(solution)/shard_map/dot_general | solution.py:54
  113.3 2.8 %fusion.2 = f32[256,1536]{1,0:T(8,128)S(1)} fusion(f32[256,512]{1,0:T(8,128)S(1)} %get-tuple-element.38, f32[512,768]{1,0:T(8,128)S(1)} %get-tuple-element.29, f32[512,768]{1,0:T(8,128)S(1)} %copy-done.17), kind=kOutput, calls=%fused_computation.6 | convolution fusion | flops 2416705536 | bytes 5242880 | tf_op jit(solution)/shard_map/dot_general | solution.py:35
  116.1 5.6 %fusion.71 = f32[1024,1536]{1,0:T(8,128)S(1)} fusion(f32[256,1536]{1,0:T(8,128)S(1)} %fusion.2, f32[256,512]{1,0:T(8,128)S(1)} %copy-done.11, f32[256,512]{1,0:T(8,128)S(1)} %copy-done.9), kind=kOutput, calls=%fused_computation.100 | convolution fusion | flops 4832100352 | bytes 8912896 | tf_op jit(solution)/shard_map/dot_general | solution.py:36
  122.9 5.8 %fusion.12 = f32[512,1536]{1,0:T(8,128)S(1)} fusion(f32[512,768]{1,0:T(8,128)S(1)} %get-tuple-element.10, f32[512,768]{1,0:T(8,128)S(1)} %get-tuple-element.9, f32[256,512]{1,0:T(8,128)S(1)} %copy-done.22, f32[256,512]{1,0:T(8,128)S(1)} %copy-done.20), kind=kOutput, calls=%fused_computation.16 | convolution fusion | flops 4832886784 | bytes 7340032 | tf_op jit(solution)/shard_map/dot_general | solution.py:47
  130.1 2.2 fusion.91
  136.0 3.9 %collective-permute-done.5 = f32[128,512]{1,0:T(8,128)S(1)} collective-permute-done((f32[128,512]{1,0:T(8,128)S(1)}, f32[128,512]{1,0:T(8,128)S(1)}, u32[]{:S(2)}, u32[]{:S(2)}) %collective-permute-start.5) | collective-permute-done | bytes 262176 | tf_op jit(solution)/shard_map/ppermute | solution.py:19
  142.4 4.1 %collective-permute-start.6 = (f32[512,128]{1,0:T(8,128)}, f32[512,128]{1,0:T(8,128)}, u32[]{:S(2)}, u32[]{:S(2)}) collective-permute-start(f32[512,128]{1,0:T(8,128)} %get-tuple-element.19), channel_id=1, source_target_pairs={{0,1},{1,2},{2,3},{4,5},{5,6},{6,7},{8,9},{9,10},{10,11},{12,13},{... | collective-permute-start | bytes 786440 | tf_op jit(solution)/shard_map/ppermute | solution.py:16
  147.8 4.9 %reduce-scatter.2.cloned.1.call-done = f32[64,256]{1,0:T(8,128)} async-done(((f32[256,256]{1,0:T(8,128)}), f32[64,256]{1,0:T(8,128)}) %reduce-scatter.2.cloned.1.call-update) | async-done | bytes 65552 | tf_op jit(solution)/shard_map/reduce_scatter | solution.py:121
  152.7 14.5 %all-gather = f32[256,256]{1,0:T(8,128)S(1)} all-gather(f32[64,256]{1,0:T(8,128)} %reduce-scatter.2.cloned.1.call-done), channel_id=2, replica_groups=mesh['groups'=2,'row'=4,'col'=4] {'col'}, dimensions={0}, use_global_device_ids=true | all-gather | bytes 327680 | tf_op jit(solution)/shard_map/all_gather | solution.py:122
  167.9 6.3 %psum.23 = f32[]{:T(128)} all-reduce(f32[]{:T(128)} %multiply_reduce_fusion.2), channel_id=1, replica_groups=mesh['groups'=2,'row'=4,'col'=4] {'row'}, use_global_device_ids=true, to_apply=%region_7.8 | all-reduce | flops 1 | bytes 8 | tf_op jit(solution)/shard_map/psum | solution.py:123
  174.2 10.7 %fusion = f32[512,1536]{1,0:T(8,128)S(1)} fusion(f32[768,768]{1,0:T(8,128)} %copy-done.24, f32[768,768]{1,0:T(8,128)} %copy-done.25, f32[512,128]{1,0:T(8,128)} %collective-permute-done.7, f32[128,512]{1,0:T(8,128)} %copy-done.29, f32[256,512]{1,0:T(8,128)} %copy-done.13, f32[128,512]{1,0:T(8,128)} %copy-done.28, f32[512,128]{1,0:T(8,128)} %collective-permute-done.6), kind=kOutput, calls=%fused_computation.1 | convolution fusion | flops 7250509824 | bytes 9437184 | tf_op jit(solution)/shard_map/dot_general | solution.py:35
  184.9 10.9 %fusion.25 = f32[1024,1536]{1,0:T(8,128)S(1)} fusion(f32[512,1536]{1,0:T(8,128)S(1)} %fusion, f32[512,512]{1,0:T(8,128)S(1)} %copy-done.6, f32[512,512]{1,0:T(8,128)S(1)} %copy-done.8), kind=kOutput, calls=%fused_computation.34 | convolution fusion | flops 9664200704 | bytes 11534336 | tf_op jit(solution)/shard_map/dot_general | solution.py:36
  197.1 5.6 %fusion.7 = f32[512,1536]{1,0:T(8,128)S(1)} fusion(f32[512,768]{1,0:T(8,128)S(1)} %get-tuple-element.12, f32[512,768]{1,0:T(8,128)S(1)} %get-tuple-element.11, f32[256,512]{1,0:T(8,128)S(1)} %copy-done.12, f32[256,512]{1,0:T(8,128)S(1)} %copy-done.10), kind=kOutput, calls=%fused_computation.11 | convolution fusion | flops 4832886784 | bytes 7340032 | tf_op jit(solution)/shard_map/dot_general | solution.py:47
  204.7 5.6 %multiply_reduce_fusion = (f32[]{:T(128)}, f32[256,512]{1,0:T(8,128)}) fusion(f32[512,768]{1,0:T(8,128)S(1)} %get-tuple-element.29, f32[512,768]{1,0:T(8,128)S(1)} %copy-done.4, f32[256,768]{1,0:T(8,128)} %get-tuple-element.16, f32[256,768]{1,0:T(8,128)} %get-tuple-element.15), kind=kOutput, calls=%fused_computation.138 | convolution fusion | flops 2417491968 | bytes 5242884 | tf_op jit(solution)/shard_map/dot_general | solution.py:54
  210.3 33.3 %all-reduce = (f32[]{:T(128)}, f32[]{:T(128)}) all-reduce(f32[]{:T(128)} %get-tuple-element.37, f32[]{:T(128)} %get-tuple-element.39), channel_id=1, replica_groups=mesh['groups'=2,'row'=4,'col'=4] {'row','col'}, use_global_device_ids=true, to_apply=%region_1.2 | all-reduce | flops 2 | bytes 16 | tf_op jit(solution)/shard_map/psum | solution.py:97
  (92 shorter events, 23.1 us)
Async XLA Ops:
  7.2 145.6 %reduce-scatter.2.cloned.1.call-start = ((), (), s32[]{:S(2)}) async-start(), calls=%async_computation.1 | async-start | bytes 327680 | tf_op jit(solution)/shard_map/reduce_scatter | solution.py:121
  8.3 55.3 %collective-permute-start = (f32[128,512]{1,0:T(8,128)S(1)}, f32[128,512]{1,0:T(8,128)S(1)}, u32[]{:S(2)}, u32[]{:S(2)}) collective-permute-start(f32[128,512]{1,0:T(8,128)S(1)} %get-tuple-element.26), channel_id=1, source_target_pairs={{0,4},{4,8},{8,12},{1,5},{5,9},{9,13},{2,6},{6,10},{10,14},{3,7},{... | collective-permute-start | bytes 786440 | tf_op jit(solution)/shard_map/ppermute | solution.py:16
  10.7 53.0 %collective-permute-start.1 = (f32[128,512]{1,0:T(8,128)S(1)}, f32[128,512]{1,0:T(8,128)S(1)}, u32[]{:S(2)}, u32[]{:S(2)}) collective-permute-start(f32[128,512]{1,0:T(8,128)S(1)} %get-tuple-element.25), channel_id=1, source_target_pairs={{4,0},{8,4},{12,8},{5,1},{9,5},{13,9},{6,2},{10,6},{14,10},{7,3},{... | collective-permute-start | bytes 786440 | tf_op jit(solution)/shard_map/ppermute | solution.py:19
  12.0 6.4 %copy-start.27 = (f32[64,256]{1,0:T(8,128)S(1)}, f32[64,256]{1,0:T(8,128)}, u32[]{:S(2)}) copy-start(f32[64,256]{1,0:T(8,128)} %param.5) | copy-start | bytes 196612
  16.2 19.6 %copy-start.14 = (f32[256,768]{1,0:T(8,128)}, f32[256,768]{1,0:T(8,128)S(1)}, u32[]{:S(2)}) copy-start(f32[256,768]{1,0:T(8,128)S(1)} %get-tuple-element.32) | copy-start | bytes 2359300
  18.4 20.2 %copy-start.19 = (f32[256,512]{1,0:T(8,128)}, f32[256,512]{1,0:T(8,128)S(1)}, u32[]{:S(2)}) copy-start(f32[256,512]{1,0:T(8,128)S(1)} %get-tuple-element.35) | copy-start | bytes 1572868
  18.4 20.2 %copy-start.21 = (f32[256,512]{1,0:T(8,128)}, f32[256,512]{1,0:T(8,128)S(1)}, u32[]{:S(2)}) copy-start(f32[256,512]{1,0:T(8,128)S(1)} %get-tuple-element.36) | copy-start | bytes 1572868
  59.0 18.4 %copy-start.24 = (f32[768,768]{1,0:T(8,128)}, f32[768,768]{1,0:T(8,128)S(1)}, u32[]{:S(2)}) copy-start(f32[768,768]{1,0:T(8,128)S(1)} %get-tuple-element.41) | copy-start | bytes 7077892
  59.1 18.4 %copy-start.25 = (f32[768,768]{1,0:T(8,128)}, f32[768,768]{1,0:T(8,128)S(1)}, u32[]{:S(2)}) copy-start(f32[768,768]{1,0:T(8,128)S(1)} %get-tuple-element.42) | copy-start | bytes 7077892
  59.1 4.6 %copy-start.18 = (f32[256,512]{1,0:T(8,128)S(1)}, f32[256,512]{1,0:T(8,128)}, u32[]{:S(2)}) copy-start(f32[256,512]{1,0:T(8,128)} %param.4) | copy-start | bytes 1572868
  63.6 21.6 %copy-start.5 = (f32[512,512]{1,0:T(8,128)}, f32[512,512]{1,0:T(8,128)S(1)}, u32[]{:S(2)}) copy-start(f32[512,512]{1,0:T(8,128)S(1)} %get-tuple-element.43) | copy-start | bytes 3145732
  63.6 21.6 %copy-start.7 = (f32[512,512]{1,0:T(8,128)}, f32[512,512]{1,0:T(8,128)S(1)}, u32[]{:S(2)}) copy-start(f32[512,512]{1,0:T(8,128)S(1)} %get-tuple-element.44) | copy-start | bytes 3145732
  63.8 9.5 %collective-permute-start.2 = (f32[512,128]{1,0:T(8,128)S(1)}, f32[512,128]{1,0:T(8,128)S(1)}, u32[]{:S(2)}, u32[]{:S(2)}) collective-permute-start(f32[512,128]{1,0:T(8,128)S(1)} %get-tuple-element.21), channel_id=1, source_target_pairs={{0,1},{1,2},{2,3},{4,5},{5,6},{6,7},{8,9},{9,10},{10,11},{12,13},{... | collective-permute-start | bytes 786440 | tf_op jit(solution)/shard_map/ppermute | solution.py:16
  67.3 10.2 %collective-permute-start.3 = (f32[512,128]{1,0:T(8,128)S(1)}, f32[512,128]{1,0:T(8,128)S(1)}, u32[]{:S(2)}, u32[]{:S(2)}) collective-permute-start(f32[512,128]{1,0:T(8,128)S(1)} %get-tuple-element.22), channel_id=1, source_target_pairs={{1,0},{2,1},{3,2},{5,4},{6,5},{7,6},{9,8},{10,9},{11,10},{13,12},{... | collective-permute-start | bytes 786440 | tf_op jit(solution)/shard_map/ppermute | solution.py:19
  99.5 2.9 %copy-start.9 = (f32[256,512]{1,0:T(8,128)S(1)}, f32[256,512]{1,0:T(8,128)}, u32[]{:S(2)}) copy-start(f32[256,512]{1,0:T(8,128)} %get-tuple-element.33) | copy-start | bytes 1572868
  99.5 2.9 %copy-start.11 = (f32[256,512]{1,0:T(8,128)S(1)}, f32[256,512]{1,0:T(8,128)}, u32[]{:S(2)}) copy-start(f32[256,512]{1,0:T(8,128)} %get-tuple-element.34) | copy-start | bytes 1572868
  99.5 3.1 %copy-start.16 = (f32[512,768]{1,0:T(8,128)S(1)}, f32[512,768]{1,0:T(8,128)}, u32[]{:S(2)}) copy-start(f32[512,768]{1,0:T(8,128)} %get-tuple-element.4) | copy-start | bytes 4718596
  108.0 1.4 copy-start.3
  108.0 1.5 copy-start.26
  109.5 3.7 %copy-start.17 = (f32[512,768]{1,0:T(8,128)S(1)}, f32[512,768]{1,0:T(8,128)}, u32[]{:S(2)}) copy-start(f32[512,768]{1,0:T(8,128)} %get-tuple-element.27) | copy-start | bytes 4718596
  113.3 2.8 %copy-start.13 = (f32[256,512]{1,0:T(8,128)}, f32[256,512]{1,0:T(8,128)S(1)}, u32[]{:S(2)}) copy-start(f32[256,512]{1,0:T(8,128)S(1)} %get-tuple-element.38) | copy-start | bytes 1572868
  116.1 5.6 %copy-start.1 = (f32[512,768]{1,0:T(8,128)S(1)}, f32[512,768]{1,0:T(8,128)}, u32[]{:S(2)}) copy-start(f32[512,768]{1,0:T(8,128)} %get-tuple-element.5) | copy-start | bytes 4718596
  116.1 5.6 %copy-start.2 = (f32[512,768]{1,0:T(8,128)S(1)}, f32[512,768]{1,0:T(8,128)}, u32[]{:S(2)}) copy-start(f32[512,768]{1,0:T(8,128)} %get-tuple-element.6) | copy-start | bytes 4718596
  133.4 2.6 %collective-permute-start.4 = (f32[128,512]{1,0:T(8,128)S(1)}, f32[128,512]{1,0:T(8,128)S(1)}, u32[]{:S(2)}, u32[]{:S(2)}) collective-permute-start(f32[128,512]{1,0:T(8,128)S(1)} %get-tuple-element.23), channel_id=1, source_target_pairs={{0,4},{4,8},{8,12},{1,5},{5,9},{9,13},{2,6},{6,10},{10,14},{3,7},{... | collective-permute-start | bytes 786440 | tf_op jit(solution)/shard_map/ppermute | solution.py:16
  134.7 5.2 %collective-permute-start.5 = (f32[128,512]{1,0:T(8,128)S(1)}, f32[128,512]{1,0:T(8,128)S(1)}, u32[]{:S(2)}, u32[]{:S(2)}) collective-permute-start(f32[128,512]{1,0:T(8,128)S(1)} %get-tuple-element.24), channel_id=1, source_target_pairs={{4,0},{8,4},{12,8},{5,1},{9,5},{13,9},{6,2},{10,6},{14,10},{7,3},{... | collective-permute-start | bytes 786440 | tf_op jit(solution)/shard_map/ppermute | solution.py:19
  136.0 11.8 %copy-start.28 = (f32[128,512]{1,0:T(8,128)}, f32[128,512]{1,0:T(8,128)S(1)}, u32[]{:S(2)}) copy-start(f32[128,512]{1,0:T(8,128)S(1)} %collective-permute-done.4) | copy-start | bytes 786436
  142.4 31.8 %collective-permute-start.6 = (f32[512,128]{1,0:T(8,128)}, f32[512,128]{1,0:T(8,128)}, u32[]{:S(2)}, u32[]{:S(2)}) collective-permute-start(f32[512,128]{1,0:T(8,128)} %get-tuple-element.19), channel_id=1, source_target_pairs={{0,1},{1,2},{2,3},{4,5},{5,6},{6,7},{8,9},{9,10},{10,11},{12,13},{... | collective-permute-start | bytes 786440 | tf_op jit(solution)/shard_map/ppermute | solution.py:16
  146.5 27.7 %collective-permute-start.7 = (f32[512,128]{1,0:T(8,128)}, f32[512,128]{1,0:T(8,128)}, u32[]{:S(2)}, u32[]{:S(2)}) collective-permute-start(f32[512,128]{1,0:T(8,128)} %get-tuple-element.20), channel_id=1, source_target_pairs={{1,0},{2,1},{3,2},{5,4},{6,5},{7,6},{9,8},{10,9},{11,10},{13,12},{... | collective-permute-start | bytes 786440 | tf_op jit(solution)/shard_map/ppermute | solution.py:19
  174.2 10.7 %copy-start.6 = (f32[512,512]{1,0:T(8,128)S(1)}, f32[512,512]{1,0:T(8,128)}, u32[]{:S(2)}) copy-start(f32[512,512]{1,0:T(8,128)} %copy-done.5) | copy-start | bytes 3145732
  174.2 10.7 %copy-start.8 = (f32[512,512]{1,0:T(8,128)S(1)}, f32[512,512]{1,0:T(8,128)}, u32[]{:S(2)}) copy-start(f32[512,512]{1,0:T(8,128)} %copy-done.7) | copy-start | bytes 3145732
  184.9 10.9 %copy-start = (f32[512,768]{1,0:T(8,128)S(1)}, f32[512,768]{1,0:T(8,128)}, u32[]{:S(2)}) copy-start(f32[512,768]{1,0:T(8,128)} %get-tuple-element.8) | copy-start | bytes 4718596
  202.7 2.0 copy-start.4
  (7 other events, 7.7 us)
Sparse Core Ops, SparseCore 0:
  132.4 20.2 reduce-scatter.1
